TPU v7x, 32 devices: a whole 2x2x4 slice. The times are simulated.
32 devices in a mesh: wa: 8 (over y, x, core), gz: 4 (over z).
Axes of the slice: x: 2, y: 2, z: 4, core: 2. Of those that a mesh axis runs over, the one named last changes fastest.
Arguments:
- velocity_modes: float32 [2, 8, 512, 512], P(None, 'gz', 'wa'), may hold values from -0.03125 to 0.03125
- scalar: float32 [16, 1024, 1024], P('gz', 'wa'), may hold values from -3 to 3
- nest_shift: int32 [1], replicated, may hold values from 0 to 1023
Outputs:
- stress: bfloat16 [2, 8, 512, 512], P(None, 'gz', 'wa')
- scalar_next: float32 [16, 1024, 1024], P('gz', 'wa')
Inputs may be any that keep to these rules, and one draw needn't show every extreme that they name: `nest_shift`: a shift of the fine grid along x in fine cells.
All inputs are finite; a program needn't handle non-finite values.
Results may differ from a plain program's by a relative error of at most 0.001.
Values sent between devices are 32-bit elements; how exact they have to be, the bound alone decides.
A program may use at most 128 MiB of HBM per device.

v0:
```python
import functools
import math

import jax
import jax.numpy as jnp
import numpy as np
from jax import lax
from jax.experimental import pallas as pl
from jax.experimental.pallas import tpu as pltpu
from jax.sharding import PartitionSpec as P

time_step = 0.2
edge = 4
margin = 16


def signed_modes(length):
    number = np.arange(length)
    return np.where(number < length // 2, number, number - length)


def hartley_table(modes, points, length):
    phase = np.mod(modes[:, None] * points[None, :], length) * (2.0 * math.pi / length)
    return (np.cos(phase) + np.sin(phase)).astype(np.float32)


def cubic_weights(fraction):
    square = fraction * fraction
    cube = square * fraction
    return (
        (-cube + 2.0 * square - fraction) * 0.5,
        (3.0 * cube - 5.0 * square + 2.0) * 0.5,
        (-3.0 * cube + 4.0 * square + fraction) * 0.5,
        (cube - square) * 0.5,
    )


def interp_matrix(lower, fraction, coarse_count):
    coarse = jnp.arange(coarse_count, dtype=jnp.int32)[:, None]
    matrix = jnp.zeros((coarse_count, lower.shape[0]), jnp.float32)
    for offset, weight in zip(range(-1, 3), cubic_weights(fraction)):
        target = jnp.mod(lower + offset, coarse_count)
        matrix = matrix + jnp.where(coarse == target[None, :], weight[None, :], 0.0)
    return matrix


def split(value):
    high = value.astype(jnp.bfloat16)
    return high, (value - high.astype(jnp.float32)).astype(jnp.bfloat16)


def dot3(left, right, contract):
    dims = (contract, ((), ()))
    product = functools.partial(
        lax.dot_general, dimension_numbers=dims, preferred_element_type=jnp.float32
    )
    return (
        product(left[0], right[1]) + product(left[1], right[0]) + product(left[0], right[0])
    )


rows_by_columns = ((1,), (0,))
rows_by_rows = ((1,), (1,))


def stress_kernel(planes, kx, block_ref, table_ref, out_ref, gathered):
    pencils = block_ref.shape[0]
    rows = out_ref.shape[1]
    table = split(table_ref[...])
    layers = planes // 2

    def spaced(plane):
        for s in range(pencils):
            gathered[:, s * kx : (s + 1) * kx] = block_ref[
                s, :rows, plane * kx : (plane + 1) * kx
            ]
        return dot3(split(gathered[...]), table, rows_by_columns)

    for layer in range(layers):
        u = spaced(layer)
        v = spaced(layers + layer)
        for c, product in ((0, u * u - v * v), (1, u * v)):
            half = dot3(split(product), table, rows_by_rows)
            plane = c * layers + layer
            for d in range(pencils):
                out_ref[d, :, plane * kx : (plane + 1) * kx] = half[:, d * kx : (d + 1) * kx]


def fine_kernel(layers, kx, own_ref, below_ref, above_ref, matrix_y_ref, synth_ref, out_ref, gathered, lines):
    pencils = own_ref.shape[0]
    synth = split(synth_ref[...])
    matrix_y = split(matrix_y_ref[...])
    for c in range(2):
        for p in range(layers + 4):
            if p < 2:
                ref, layer = below_ref, layers - 2 + p
            elif p < 2 + layers:
                ref, layer = own_ref, p - 2
            else:
                ref, layer = above_ref, p - 2 - layers
            plane = c * layers + layer
            for s in range(pencils):
                gathered[:, s * kx : (s + 1) * kx] = ref[s, :, plane * kx : (plane + 1) * kx]
            lines[p] = dot3(matrix_y, split(gathered[...]), rows_by_columns)
        for k in range(-1, 2 * layers + 1):
            lower = (2 * k - 1) // 4
            weights = cubic_weights(((2 * k - 1) % 4) / 4.0)
            mixed = weights[0] * lines[lower + 1]
            for offset in range(1, 4):
                mixed = mixed + weights[offset] * lines[lower + 1 + offset]
            out_ref[c, k + 1] = dot3(split(mixed), synth, rows_by_columns)


def heun_kernel(own_ref, before_ref, after_ref, below_ref, above_ref, speed_ref, out_ref, field, section):
    layers, rows, width = own_ref.shape
    end = margin + rows
    for z in range(layers):
        field[z + 2, margin:end] = own_ref[z]
        field[z + 2, margin - 2 : margin] = before_ref[z]
        field[z + 2, end : end + 2] = after_ref[z]
    for z in range(2):
        for at, ref in ((z, below_ref), (z + layers + 2, above_ref)):
            field[at, margin:end] = ref[z, :rows]
            field[at, end : end + 2] = ref[z, rows : rows + 2]
            field[at, margin - 2 : margin] = ref[z, rows + 2 : rows + 4]

    def rate(source, z, row, speed_z):
        middle = source[z, pl.ds(row, 8), :]
        previous = source[z, pl.ds(row - 8, 8), :]
        following = source[z, pl.ds(row + 8, 8), :]
        sublane = lax.broadcasted_iota(jnp.int32, (8, width), 0)
        north = pltpu.roll(jnp.where(sublane == 0, following, middle), 7, 0)
        south = pltpu.roll(jnp.where(sublane == 7, previous, middle), 1, 0)
        east = pltpu.roll(middle, width - 1, 1)
        west = pltpu.roll(middle, 1, 1)
        speed_row = row - (margin - 8)
        tendency = (-0.5 * speed_ref[0, speed_z, pl.ds(speed_row, 8), :]) * (east - west)
        tendency = tendency - (0.5 * speed_ref[1, speed_z, pl.ds(speed_row, 8), :]) * (north - south)
        base = 2.0 + middle * middle
        upper = source[z + 1, pl.ds(row, 8), :]
        lower = source[z - 1, pl.ds(row, 8), :]
        flux = None
        for other in (east, west, north, south, upper, lower):
            term = (base + other * other) * (other - middle)
            flux = term if flux is None else flux + term
        return middle, tendency + 0.05 * flux

    first_chunks = rows // 8 + 2

    def first(step, _):
        z = step // first_chunks + 1
        row = pl.multiple_of((step % first_chunks) * 8 + margin - 8, 8)
        middle, tendency = rate(field, z, row, z - 1)
        section[z - 1, pl.ds(row, 8), :] = middle + time_step * tendency
        return 0

    lax.fori_loop(0, (layers + 2) * first_chunks, first, 0)
    chunks = rows // 8

    def second(step, _):
        z = step // chunks
        row = pl.multiple_of((step % chunks) * 8 + margin, 8)
        middle, tendency = rate(section, z + 1, row, z + 1)
        own = own_ref[z, pl.ds(row - margin, 8), :]
        out_ref[z, pl.ds(row - margin, 8), :] = 0.5 * (own + middle + time_step * tendency)
        return 0

    lax.fori_loop(0, layers * chunks, second, 0)


def in_vmem(kernel, shape, count, scratch, flops):
    spec = pl.BlockSpec(memory_space=pltpu.VMEM)
    return pl.pallas_call(
        kernel,
        out_shape=jax.ShapeDtypeStruct(shape, jnp.float32),
        in_specs=[spec] * count,
        out_specs=spec,
        scratch_shapes=scratch,
        compiler_params=pltpu.CompilerParams(vmem_limit_bytes=56 * 1024 * 1024),
        cost_estimate=pl.CostEstimate(flops=flops, bytes_accessed=4 * 1024 * 1024, transcendentals=0),
    )


def shards(velocity_modes, scalar, nest_shift):
    pencils = lax.axis_size("wa")
    slabs = lax.axis_size("gz")
    _, layers, kx, ky_count = velocity_modes.shape
    kx_count = kx * pencils
    fine_layers, fine_rows, fine_x = scalar.shape
    padded_x = 3 * kx_count // 2
    padded_y = 3 * ky_count // 2
    y_local = padded_y // pencils
    rows = y_local + 2 * edge
    planes = 2 * layers

    order = np.concatenate([np.arange(y_local + edge), np.arange(-edge, 0)])
    y_points = (y_local * np.arange(pencils)[:, None] + order[None, :]).reshape(-1) % padded_y
    synth_y = jnp.asarray(hartley_table(signed_modes(ky_count), y_points, padded_y)).reshape(
        ky_count, pencils, rows
    )
    analysis_y = jnp.asarray(
        hartley_table(signed_modes(ky_count), np.arange(padded_y), padded_y)
    ).reshape(ky_count, pencils, y_local)
    synth_x = jnp.asarray(hartley_table(signed_modes(kx_count), np.arange(padded_x), padded_x))

    speed_rows = fine_rows + 16
    matrix_y = np.zeros((speed_rows, rows), np.float32)
    place = {int(r): i for i, r in enumerate(order)}
    for j in range(-1, fine_rows + 1):
        numer = 3 * (2 * j + 1)
        for offset, weight in zip(range(-1, 3), cubic_weights((numer % 8) / 8.0)):
            matrix_y[j + 8, place[numer // 8 + offset]] += weight

    def ring(axis, count, value, step):
        return lax.ppermute(value, axis, [(i, (i + step) % count) for i in range(count)])

    modes_below = ring("gz", slabs, velocity_modes, 1)
    modes_above = ring("gz", slabs, velocity_modes, -1)
    before = ring("wa", pencils, scalar[:, -2:], 1)
    after = ring("wa", pencils, scalar[:, :2], -1)

    def to_rows(modes):
        lines = jnp.einsum(
            "nq,qdr->drn", modes.reshape(planes * kx, ky_count), synth_y, precision=lax.Precision.HIGH
        )
        return lax.all_to_all(lines, "wa", split_axis=0, concat_axis=0, tiled=True)

    own = to_rows(velocity_modes)
    half_done = in_vmem(
        functools.partial(stress_kernel, planes, kx),
        (pencils, y_local, planes * kx),
        2,
        [pltpu.VMEM((y_local, kx_count), jnp.float32)],
        12 * planes * y_local * kx_count * padded_x,
    )(own, synth_x)
    returned = lax.all_to_all(half_done, "wa", split_axis=0, concat_axis=0, tiled=True)
    stress = jnp.einsum("syn,qsy->nq", returned, analysis_y, precision=lax.Precision.HIGH)
    stress = (stress * (1.0 / math.sqrt(padded_x * padded_y))).astype(jnp.bfloat16)
    stress = stress.reshape(2, layers, kx, ky_count)

    numer_x = 3 * (2 * jnp.arange(fine_x, dtype=jnp.int32) + 1 + 2 * nest_shift[0])
    matrix_x = interp_matrix(numer_x // 8, (numer_x % 8).astype(jnp.float32) / 8.0, padded_x)
    synth_fine = jnp.dot(synth_x, matrix_x, precision=lax.Precision.HIGH)

    top = jnp.concatenate([scalar[-2:], after[-2:], before[-2:]], axis=1)
    bottom = jnp.concatenate([scalar[:2], after[:2], before[:2]], axis=1)
    below = ring("gz", slabs, top, 1)
    above = ring("gz", slabs, bottom, -1)

    speed = in_vmem(
        functools.partial(fine_kernel, layers, kx),
        (2, fine_layers + 2, speed_rows, fine_x),
        5,
        [
            pltpu.VMEM((rows, kx_count), jnp.float32),
            pltpu.VMEM((layers + 4, speed_rows, kx_count), jnp.float32),
        ],
        12 * (fine_layers + 2) * speed_rows * kx_count * fine_x,
    )(own, to_rows(modes_below), to_rows(modes_above), jnp.asarray(matrix_y), synth_fine)

    scalar_next = in_vmem(
        heun_kernel,
        scalar.shape,
        6,
        [
            pltpu.VMEM((fine_layers + 4, fine_rows + 2 * margin, fine_x), jnp.float32),
            pltpu.VMEM((fine_layers + 2, fine_rows + 2 * margin, fine_x), jnp.float32),
        ],
        100 * fine_layers * fine_rows * fine_x,
    )(scalar, before, after, below, above, speed)
    return (stress, scalar_next)


def solution(mesh):
    placed = (P(None, "gz", "wa", None), P("gz", "wa", None), P())
    return jax.shard_map(
        shards,
        mesh=mesh,
        in_specs=placed,
        out_specs=(P(None, "gz", "wa", None), P("gz", "wa", None)),
        check_vma=False,
    )
```

profile of v0, /device:TPU:0, one launch (start us, length us, event | category | flops | bytes accessed | tf_op | source)
XLA Modules:
  0.0 130.0 jit_solution(7713257723209074623)
XLA Ops:
  0.6 3.1 %collective-permute-start.4 = (f32[2,2,64,512]{3,2,1,0:T(8,128)}, f32[2,2,64,512]{3,2,1,0:T(8,128)}, u32[]{:S(2)}, u32[]{:S(2)}) collective-permute-start(f32[2,2,64,512]{3,2,1,0:T(8,128)} %param.7), channel_id=1, source_target_pairs={{0,1},{1,2},{2,3},{3,0},{4,5},{5,6},{6,7},{7,4},{8,9},{9,10},{10,1... | collective-permute-start | bytes 1572872 | tf_op jit(solution)/shard_map/ppermute | solution.py:215
  3.7 2.1 %collective-permute-start.5 = (f32[2,2,64,512]{3,2,1,0:T(8,128)}, f32[2,2,64,512]{3,2,1,0:T(8,128)S(1)}, u32[]{:S(2)}, u32[]{:S(2)}) collective-permute-start(f32[2,2,64,512]{3,2,1,0:T(8,128)} %param.7), channel_id=1, source_target_pairs={{0,3},{1,0},{2,1},{3,2},{4,7},{5,4},{6,5},{7,6},{8,11},{9,8},{10,9... | collective-permute-start | bytes 1572872 | tf_op jit(solution)/shard_map/ppermute | solution.py:215
  5.8 0.0 copy-start.1
  5.8 3.5 %fusion.42 = f32[8,104,256]{2,1,0:T(8,128)} fusion(f32[512,8,104]{0,2,1:T(8,128)} %constant.82, f32[256,512,1]{1,0,2:T(8,128)} %bitcast.26), kind=kOutput, calls=%fused_computation.68 | convolution fusion | flops 654311424 | bytes 3080192 | tf_op jit(solution)/shard_map/nq,qdr->drn/dot_general | solution.py:223
  9.3 4.2 %all-to-all-start = ((f32[8,104,256]{2,1,0:T(8,128)}), f32[8,104,256]{2,1,0:T(8,128)}, u32[]{:S(2)}, u32[]{:S(2)}) async-start(f32[8,104,256]{2,1,0:T(8,128)} %fusion.42), calls=%async_computation | async-start | bytes 1703936 | tf_op jit(solution)/shard_map/all_to_all | solution.py:226
  13.6 0.0 copy-done.1
  13.6 2.6 %collective-permute-start.1 = (f32[4,2,1024]{2,1,0:T(2,128)S(1)}, f32[4,2,1024]{2,1,0:T(2,128)S(1)}, u32[]{:S(2)}, u32[]{:S(2)}) collective-permute-start(f32[4,2,1024]{2,1,0:T(2,128)S(1)} %get-tuple-element.4), channel_id=1, source_target_pairs={{0,28},{4,0},{8,4},{12,8},{16,12},{20,16},{24,20},{28,24},{1,29},{... | collective-permute-start | bytes 98312 | tf_op jit(solution)/shard_map/ppermute | solution.py:215
  16.2 0.0 collective-permute-start
  16.9 0.2 fusion.38
  17.1 0.0 copy-start
  17.1 1.8 %copy.17 = f32[2,128,1024]{2,0,1:T(2,128)} copy(f32[2,128,1024]{2,1,0:T(8,128)S(1)} %get-tuple-element.3) | data formatting | bytes 2097152
  18.9 0.8 copy.18
  19.7 0.0 collective-permute-done.4
  19.7 0.0 copy-done
  19.7 2.8 %fusion.43 = f32[8,104,256]{2,1,0:T(8,128)} fusion(f32[512,8,104]{0,2,1:T(8,128)S(1)} %copy-done, f32[256,512,1]{1,0,2:T(8,128)} %bitcast.5), kind=kOutput, calls=%fused_computation.69 | convolution fusion | flops 654311424 | bytes 3080192 | tf_op jit(solution)/shard_map/nq,qdr->drn/dot_general | solution.py:223
  22.6 4.6 %all-to-all-done.block_ref.own_ref = f32[8,104,256]{2,1,0:T(8,128)} async-done(((f32[8,104,256]{2,1,0:T(8,128)}), f32[8,104,256]{2,1,0:T(8,128)}, u32[]{:S(2)}, u32[]{:S(2)}) %all-to-all-start) | async-done | bytes 852000 | tf_op jit(solution)/shard_map/all_to_all | solution.py:226
  27.2 4.2 %all-to-all-start.2 = ((f32[8,104,256]{2,1,0:T(8,128)}), f32[8,104,256]{2,1,0:T(8,128)}, u32[]{:S(2)}, u32[]{:S(2)}) async-start(f32[8,104,256]{2,1,0:T(8,128)} %fusion.43), calls=%async_computation.2 | async-start | bytes 1703936 | tf_op jit(solution)/shard_map/all_to_all | solution.py:226
  31.4 0.0 collective-permute-done.1.after_ref
  31.5 0.0 copy-start.3
  31.5 0.0 collective-permute-done.before_ref
  31.5 0.0 copy-start.4
  31.6 2.7 %pad_maximum_fusion = f32[2,132,1024]{2,0,1:T(2,128)} fusion(f32[2,2,1024]{2,0,1:T(2,128)S(1)} %copy.11, f32[2,2,1024]{2,0,1:T(2,128)S(1)} %copy.10, f32[2,128,1024]{2,0,1:T(2,128)} %copy.17), kind=kLoop, calls=%fused_computation.24 | loop fusion | flops 540672 | bytes 2162688 | tf_op jit(solution)/shard_map/concatenate | solution.py:245
  34.2 0.0 collective-permute-start.2
  34.3 0.0 collective-permute-done.5
  34.3 1.8 %fusion.44 = f32[8,104,256]{2,1,0:T(8,128)} fusion(f32[512,8,104]{0,2,1:T(8,128)S(1)} %copy-done, f32[256,512,1]{1,0,2:T(8,128)S(1)} %bitcast.27), kind=kOutput, calls=%fused_computation.70 | convolution fusion | flops 654311424 | bytes 3080192 | tf_op jit(solution)/shard_map/nq,qdr->drn/dot_general | solution.py:223
  36.0 0.0 copy-done.3
  36.0 0.0 copy-done.4
  36.1 8.7 %all-to-all-done.2.below_ref = f32[8,104,256]{2,1,0:T(8,128)} async-done(((f32[8,104,256]{2,1,0:T(8,128)}), f32[8,104,256]{2,1,0:T(8,128)}, u32[]{:S(2)}, u32[]{:S(2)}) %all-to-all-start.2) | async-done | bytes 852000 | tf_op jit(solution)/shard_map/all_to_all | solution.py:226
  44.7 4.2 %all-to-all-start.3 = ((f32[8,104,256]{2,1,0:T(8,128)}), f32[8,104,256]{2,1,0:T(8,128)}, u32[]{:S(2)}, u32[]{:S(2)}) async-start(f32[8,104,256]{2,1,0:T(8,128)} %fusion.44), calls=%async_computation.3 | async-start | bytes 1703936 | tf_op jit(solution)/shard_map/all_to_all | solution.py:226
  49.0 0.5 pad_maximum_fusion.1
  49.4 6.6 %collective-permute-start.3 = (f32[2,132,1024]{2,0,1:T(2,128)S(1)}, f32[2,132,1024]{2,0,1:T(2,128)S(1)}, u32[]{:S(2)}, u32[]{:S(2)}) collective-permute-start(f32[2,132,1024]{2,0,1:T(2,128)S(1)} %pad_maximum_fusion.1), channel_id=1, source_target_pairs={{0,3},{1,0},{2,1},{3,2},{4,7},{5,4},{6,5},{7,6},{8,11},{9,8},{10,9... | collective-permute-start | bytes 3244040 | tf_op jit(solution)/shard_map/ppermute | solution.py:215
  56.2 7.2 %shard_map.86 = f32[8,96,256]{2,1,0:T(8,128)} custom-call(f32[8,104,256]{2,1,0:T(8,128)} %all-to-all-done.block_ref.own_ref, f32[512,768]{1,0:T(8,128)} %constant.79.clone.table_ref), custom_call_target="tpu_custom_call" | custom-call | flops 1811939328 | bytes 4194304 | tf_op jit(solution)/shard_map/pallas_call | solution.py:229
  63.3 0.0 all-to-all-done.3.above_ref
  63.3 4.1 %all-to-all-start.1 = ((f32[8,96,256]{2,1,0:T(8,128)}), f32[8,96,256]{2,1,0:T(8,128)S(1)}, u32[]{:S(2)}, u32[]{:S(2)}) async-start(f32[8,96,256]{2,1,0:T(8,128)} %shard_map.86), calls=%async_computation.1 | async-start | bytes 1572864 | tf_op jit(solution)/shard_map/all_to_all | solution.py:236
  67.4 6.5 %fusion.synth_ref = f32[512,1024]{1,0:T(8,128)} fusion(f32[512,768]{1,0:T(8,128)} %constant.79.clone.table_ref, f32[1024]{0:T(1024)S(1)} %get-tuple-element.17, s32[1024]{0:T(1024)S(1)} %get-tuple-element.10, f32[1024]{0:T(1024)S(1)} %get-tuple-element.16, s32[1024]{0:T(1024)S(1)} %get-tuple-element.11, f32[1024]{0:T(1024)S(1)} %get-tuple-element.15, ...), kind=kOutput, calls=%fused_computation | convolution fusion | flops 2424569856 | bytes 3702784 | tf_op jit(solution)/shard_map/dot_general | solution.py:243
  74.0 0.0 collective-permute-done.2
  74.0 2.6 %copy.15.below_ref = f32[2,132,1024]{2,1,0:T(8,128)} copy(f32[2,132,1024]{2,0,1:T(2,128)} %collective-permute-done.2) | data formatting | bytes 2162688 | tf_op jit(solution)/shard_map/ppermute | solution.py:215
  76.6 12.0 %collective-permute-done.3 = f32[2,132,1024]{2,0,1:T(2,128)S(1)} collective-permute-done((f32[2,132,1024]{2,0,1:T(2,128)S(1)}, f32[2,132,1024]{2,0,1:T(2,128)S(1)}, u32[]{:S(2)}, u32[]{:S(2)}) %collective-permute-start.3) | collective-permute-done | bytes 1081376 | tf_op jit(solution)/shard_map/ppermute | solution.py:215
  88.6 1.4 %copy.16.above_ref = f32[2,132,1024]{2,1,0:T(8,128)} copy(f32[2,132,1024]{2,0,1:T(2,128)S(1)} %collective-permute-done.3) | data formatting | bytes 2162688 | tf_op jit(solution)/shard_map/ppermute | solution.py:215
  90.0 12.8 %shard_map.87.speed_ref = f32[2,6,144,1024]{3,2,1,0:T(8,128)} custom-call(f32[8,104,256]{2,1,0:T(8,128)} %all-to-all-done.block_ref.own_ref, f32[8,104,256]{2,1,0:T(8,128)} %all-to-all-done.2.below_ref, f32[8,104,256]{2,1,0:T(8,128)} %all-to-all-done.3.above_ref, f32[144,104]{1,0:T(8,128)} %constant.80.clone.matrix_y_ref, f32[512,1024]{1,0:T(8,128)} %fusion.synth_ref), custom_call_target="tpu_custom_call" | custom-call | flops 5435817984 | bytes 4194304 | tf_op jit(solution)/shard_map/pallas_call | solution.py:250
  102.8 0.0 copy-start.2
  102.8 25.7 %shard_map.88 = f32[4,128,1024]{2,1,0:T(8,128)} custom-call(f32[4,128,1024]{2,1,0:T(8,128)} %own_ref.1, f32[4,2,1024]{2,1,0:T(2,128)} %copy-done.4, f32[4,2,1024]{2,1,0:T(2,128)} %copy-done.3, f32[2,132,1024]{2,1,0:T(8,128)} %copy.15.below_ref, f32[2,132,1024]{2,1,0:T(8,128)} %copy.16.above_ref, f32[2,6,144,1024]{3,2,1,0:T(8,128)} %shard_map.87.speed_ref), custom_call_target="tpu_custom_call" | custom-call | flops 52428800 | bytes 4194304 | tf_op jit(solution)/shard_map/pallas_call | solution.py:261
  128.5 0.0 all-to-all-done.1
  128.5 0.0 copy-done.2
  128.5 1.5 %fusion.18 = bf16[256,512]{1,0:T(8,128)(2,1)} fusion(f32[8,96,256]{2,1,0:T(8,128)S(1)} %all-to-all-done.1, f32[512,8,96]{0,2,1:T(8,128)S(1)} %copy-done.2), kind=kOutput, calls=%fused_computation.23 | convolution fusion | flops 604241920 | bytes 2621440 | tf_op jit(solution)/shard_map/syn,qsy->nq/dot_general | solution.py:237
  (11 shorter events, 0.2 us)
Async XLA Ops:
  0.6 19.1 %collective-permute-start.4 = (f32[2,2,64,512]{3,2,1,0:T(8,128)}, f32[2,2,64,512]{3,2,1,0:T(8,128)}, u32[]{:S(2)}, u32[]{:S(2)}) collective-permute-start(f32[2,2,64,512]{3,2,1,0:T(8,128)} %param.7), channel_id=1, source_target_pairs={{0,1},{1,2},{2,3},{3,0},{4,5},{5,6},{6,7},{7,4},{8,9},{9,10},{10,1... | collective-permute-start | bytes 1572872 | tf_op jit(solution)/shard_map/ppermute | solution.py:215
  3.7 30.5 %collective-permute-start.5 = (f32[2,2,64,512]{3,2,1,0:T(8,128)}, f32[2,2,64,512]{3,2,1,0:T(8,128)S(1)}, u32[]{:S(2)}, u32[]{:S(2)}) collective-permute-start(f32[2,2,64,512]{3,2,1,0:T(8,128)} %param.7), channel_id=1, source_target_pairs={{0,3},{1,0},{2,1},{3,2},{4,7},{5,4},{6,5},{7,6},{8,11},{9,8},{10,9... | collective-permute-start | bytes 1572872 | tf_op jit(solution)/shard_map/ppermute | solution.py:215
  5.8 7.7 %copy-start.1 = (f32[4,128,1024]{2,1,0:T(8,128)S(1)}, f32[4,128,1024]{2,1,0:T(8,128)}, u32[]{:S(2)}) copy-start(f32[4,128,1024]{2,1,0:T(8,128)} %own_ref.1) | copy-start | bytes 6291460
  9.3 17.9 %all-to-all-start = ((f32[8,104,256]{2,1,0:T(8,128)}), f32[8,104,256]{2,1,0:T(8,128)}, u32[]{:S(2)}, u32[]{:S(2)}) async-start(f32[8,104,256]{2,1,0:T(8,128)} %fusion.42), calls=%async_computation | async-start | bytes 1703936 | tf_op jit(solution)/shard_map/all_to_all | solution.py:226
  13.6 17.8 %collective-permute-start.1 = (f32[4,2,1024]{2,1,0:T(2,128)S(1)}, f32[4,2,1024]{2,1,0:T(2,128)S(1)}, u32[]{:S(2)}, u32[]{:S(2)}) collective-permute-start(f32[4,2,1024]{2,1,0:T(2,128)S(1)} %get-tuple-element.4), channel_id=1, source_target_pairs={{0,28},{4,0},{8,4},{12,8},{16,12},{20,16},{24,20},{28,24},{1,29},{... | collective-permute-start | bytes 98312 | tf_op jit(solution)/shard_map/ppermute | solution.py:215
  16.2 15.3 %collective-permute-start = (f32[4,2,1024]{2,1,0:T(2,128)S(1)}, f32[4,2,1024]{2,1,0:T(2,128)S(1)}, u32[]{:S(2)}, u32[]{:S(2)}) collective-permute-start(f32[4,2,1024]{2,1,0:T(2,128)S(1)} %get-tuple-element.5), channel_id=1, source_target_pairs={{0,4},{4,8},{8,12},{12,16},{16,20},{20,24},{24,28},{28,0},{1,5},{5... | collective-permute-start | bytes 98312 | tf_op jit(solution)/shard_map/ppermute | solution.py:215
  17.1 2.6 %copy-start = (f32[512,8,104]{0,2,1:T(8,128)S(1)}, f32[512,8,104]{0,2,1:T(8,128)}, u32[]{:S(2)}) copy-start(f32[512,8,104]{0,2,1:T(8,128)} %constant.82) | copy-start | bytes 5111812
  27.2 17.5 %all-to-all-start.2 = ((f32[8,104,256]{2,1,0:T(8,128)}), f32[8,104,256]{2,1,0:T(8,128)}, u32[]{:S(2)}, u32[]{:S(2)}) async-start(f32[8,104,256]{2,1,0:T(8,128)} %fusion.43), calls=%async_computation.2 | async-start | bytes 1703936 | tf_op jit(solution)/shard_map/all_to_all | solution.py:226
  31.5 4.6 %copy-start.3 = (f32[4,2,1024]{2,1,0:T(2,128)}, f32[4,2,1024]{2,1,0:T(2,128)S(1)}, u32[]{:S(2)}) copy-start(f32[4,2,1024]{2,1,0:T(2,128)S(1)} %collective-permute-done.1.after_ref) | copy-start | bytes 98308
  31.5 4.5 %copy-start.4 = (f32[4,2,1024]{2,1,0:T(2,128)}, f32[4,2,1024]{2,1,0:T(2,128)S(1)}, u32[]{:S(2)}) copy-start(f32[4,2,1024]{2,1,0:T(2,128)S(1)} %collective-permute-done.before_ref) | copy-start | bytes 98308
  34.2 39.8 %collective-permute-start.2 = (f32[2,132,1024]{2,0,1:T(2,128)}, f32[2,132,1024]{2,0,1:T(2,128)}, u32[]{:S(2)}, u32[]{:S(2)}) collective-permute-start(f32[2,132,1024]{2,0,1:T(2,128)} %pad_maximum_fusion), channel_id=1, source_target_pairs={{0,1},{1,2},{2,3},{3,0},{4,5},{5,6},{6,7},{7,4},{8,9},{9,10},{10,1... | collective-permute-start | bytes 3244040 | tf_op jit(solution)/shard_map/ppermute | solution.py:215
  44.7 18.6 %all-to-all-start.3 = ((f32[8,104,256]{2,1,0:T(8,128)}), f32[8,104,256]{2,1,0:T(8,128)}, u32[]{:S(2)}, u32[]{:S(2)}) async-start(f32[8,104,256]{2,1,0:T(8,128)} %fusion.44), calls=%async_computation.3 | async-start | bytes 1703936 | tf_op jit(solution)/shard_map/all_to_all | solution.py:226
  49.4 39.2 %collective-permute-start.3 = (f32[2,132,1024]{2,0,1:T(2,128)S(1)}, f32[2,132,1024]{2,0,1:T(2,128)S(1)}, u32[]{:S(2)}, u32[]{:S(2)}) collective-permute-start(f32[2,132,1024]{2,0,1:T(2,128)S(1)} %pad_maximum_fusion.1), channel_id=1, source_target_pairs={{0,3},{1,0},{2,1},{3,2},{4,7},{5,4},{6,5},{7,6},{8,11},{9,8},{10,9... | collective-permute-start | bytes 3244040 | tf_op jit(solution)/shard_map/ppermute | solution.py:215
  63.3 65.2 %all-to-all-start.1 = ((f32[8,96,256]{2,1,0:T(8,128)}), f32[8,96,256]{2,1,0:T(8,128)S(1)}, u32[]{:S(2)}, u32[]{:S(2)}) async-start(f32[8,96,256]{2,1,0:T(8,128)} %shard_map.86), calls=%async_computation.1 | async-start | bytes 1572864 | tf_op jit(solution)/shard_map/all_to_all | solution.py:236
  102.8 25.7 %copy-start.2 = (f32[512,8,96]{0,2,1:T(8,128)S(1)}, f32[512,8,96]{0,2,1:T(8,128)}, u32[]{:S(2)}) copy-start(f32[512,8,96]{0,2,1:T(8,128)} %constant.83) | copy-start | bytes 4718596
where the time goes:
time: 131 us; the launch traced here: 130 us
  Pallas kernels  45.7 us (35%)
  starting transfers between devices  31.2 us (24%)
  waiting for transfers between devices  25.3 us (19%)
  matrix products  16.2 us (12%)
  local copies, waits for them, and re-layouts  6.96 us (5%)
  other arithmetic  3.23 us (2%)
  between operations  1.47 us (1%)
    pallas_call x1, Pallas kernels, shards(): in_vmem(heun_kernel, scalar.shape, 6, [pltpu.VMEM((fine_layers + 4, fine_...  25.7 us
    ppermute x6, starting transfers between devices, ring(): lax.ppermute(value, axis, [(i, (i + step) % count) for i in range(count)])  14.4 us
    all_to_all x3, waiting for transfers between devices, to_rows(): return lax.all_to_all(lines, 'wa', split_axis=0, concat_axis=0, tiled=True)  13.3 us
    pallas_call x1, Pallas kernels, shards(): in_vmem(functools.partial(fine_kernel, layers, kx), (2, fine_layers + 2,...  12.8 us
    all_to_all x3, starting transfers between devices, to_rows(): return lax.all_to_all(lines, 'wa', split_axis=0, concat_axis=0, tiled=True)  12.7 us
    ppermute x6, waiting for transfers between devices, ring(): lax.ppermute(value, axis, [(i, (i + step) % count) for i in range(count)])  12 us
    dot_general x3, matrix products, to_rows(): jnp.einsum('nq,qdr->drn', modes.reshape(planes * kx, ky_count), synth_y,...  8.1 us
    pallas_call x1, Pallas kernels, shards(): in_vmem(functools.partial(stress_kernel, planes, kx), (pencils, y_local,...  7.17 us
  transfers between devices with their start and end apart: 10, of which 3 were waited for; matrix products, arithmetic and copies ran while one was open for 19% of the time, Pallas kernels for 35%

commit v1 on v0

--- a/solution.py
+++ b/solution.py
@@ -8,6 +8,7 @@
 from jax.experimental import pallas as pl
 from jax.experimental.pallas import tpu as pltpu
 from jax.sharding import PartitionSpec as P
+
 
 time_step = 0.2
 edge = 4
@@ -86,29 +87,38 @@
                 out_ref[d, :, plane * kx : (plane + 1) * kx] = half[:, d * kx : (d + 1) * kx]
 
 
-def fine_kernel(layers, kx, own_ref, below_ref, above_ref, matrix_y_ref, synth_ref, out_ref, gathered, lines):
+def fine_kernel(layers, kx, own_ref, halo_ref, matrix_y_ref, synth_ref, out_ref, gathered, lines):
     pencils = own_ref.shape[0]
     synth = split(synth_ref[...])
     matrix_y = split(matrix_y_ref[...])
     for c in range(2):
         for p in range(layers + 4):
             if p < 2:
-                ref, layer = below_ref, layers - 2 + p
+                ref, plane = halo_ref, c * layers + layers - 2 + p
             elif p < 2 + layers:
-                ref, layer = own_ref, p - 2
+                ref, plane = own_ref, c * layers + p - 2
             else:
-                ref, layer = above_ref, p - 2 - layers
-            plane = c * layers + layer
+                ref, plane = halo_ref, (2 + c) * layers + p - 2 - layers
             for s in range(pencils):
                 gathered[:, s * kx : (s + 1) * kx] = ref[s, :, plane * kx : (plane + 1) * kx]
             lines[p] = dot3(matrix_y, split(gathered[...]), rows_by_columns)
         for k in range(-1, 2 * layers + 1):
             lower = (2 * k - 1) // 4
-            weights = cubic_weights(((2 * k - 1) % 4) / 4.0)
+            weights = [-0.5 * time_step * w for w in cubic_weights(((2 * k - 1) % 4) / 4.0)]
             mixed = weights[0] * lines[lower + 1]
             for offset in range(1, 4):
                 mixed = mixed + weights[offset] * lines[lower + 1 + offset]
             out_ref[c, k + 1] = dot3(split(mixed), synth, rows_by_columns)
+
+
+def pack_kernel(scalar_ref, before_ref, after_ref, top_ref, bottom_ref):
+    layers, rows, _ = scalar_ref.shape
+    for z in range(2):
+        for source, ref in ((layers - 2 + z, top_ref), (z, bottom_ref)):
+            ref[z * rows : (z + 1) * rows] = scalar_ref[source]
+            side = 2 * rows + 4 * z
+            ref[side : side + 2] = after_ref[source]
+            ref[side + 2 : side + 4] = before_ref[source]
 
 
 def heun_kernel(own_ref, before_ref, after_ref, below_ref, above_ref, speed_ref, out_ref, field, section):
@@ -120,63 +130,73 @@
         field[z + 2, end : end + 2] = after_ref[z]
     for z in range(2):
         for at, ref in ((z, below_ref), (z + layers + 2, above_ref)):
-            field[at, margin:end] = ref[z, :rows]
-            field[at, end : end + 2] = ref[z, rows : rows + 2]
-            field[at, margin - 2 : margin] = ref[z, rows + 2 : rows + 4]
-
-    def rate(source, z, row, speed_z):
-        middle = source[z, pl.ds(row, 8), :]
-        previous = source[z, pl.ds(row - 8, 8), :]
-        following = source[z, pl.ds(row + 8, 8), :]
-        sublane = lax.broadcasted_iota(jnp.int32, (8, width), 0)
-        north = pltpu.roll(jnp.where(sublane == 0, following, middle), 7, 0)
-        south = pltpu.roll(jnp.where(sublane == 7, previous, middle), 1, 0)
-        east = pltpu.roll(middle, width - 1, 1)
-        west = pltpu.roll(middle, 1, 1)
-        speed_row = row - (margin - 8)
-        tendency = (-0.5 * speed_ref[0, speed_z, pl.ds(speed_row, 8), :]) * (east - west)
-        tendency = tendency - (0.5 * speed_ref[1, speed_z, pl.ds(speed_row, 8), :]) * (north - south)
+            side = 2 * rows + 4 * z
+            field[at, margin:end] = ref[z * rows : (z + 1) * rows]
+            field[at, end : end + 2] = ref[side : side + 2]
+            field[at, margin - 2 : margin] = ref[side + 2 : side + 4]
+    sublane = lax.broadcasted_iota(jnp.int32, (8, width), 0)
+
+    def sweep(source, depth, row, speed_at, store):
+        speed_row = pl.multiple_of(row - (margin - 8), 8)
+        lower = source[0, pl.ds(row, 8), :]
+        middle = source[1, pl.ds(row, 8), :]
         base = 2.0 + middle * middle
-        upper = source[z + 1, pl.ds(row, 8), :]
-        lower = source[z - 1, pl.ds(row, 8), :]
-        flux = None
-        for other in (east, west, north, south, upper, lower):
-            term = (base + other * other) * (other - middle)
-            flux = term if flux is None else flux + term
-        return middle, tendency + 0.05 * flux
-
-    first_chunks = rows // 8 + 2
+        difference = middle - lower
+        below = (base + lower * lower) * difference
+        for z in range(1, depth - 1):
+            upper = source[z + 1, pl.ds(row, 8), :]
+            square = upper * upper
+            above = (base + square) * (upper - middle)
+            flux = above - below
+            previous = source[z, pl.ds(row - 8, 8), :]
+            following = source[z, pl.ds(row + 8, 8), :]
+            north = pltpu.roll(jnp.where(sublane == 0, following, middle), 7, 0)
+            south = pltpu.roll(jnp.where(sublane == 7, previous, middle), 1, 0)
+            flux = flux + (base + north * north) * (north - middle)
+            flux = flux + (base + south * south) * (south - middle)
+            tendency = speed_ref[1, z + speed_at, pl.ds(speed_row, 8), :] * (north - south)
+            east = pltpu.roll(middle, width - 1, 1)
+            west = pltpu.roll(middle, 1, 1)
+            face = (base + east * east) * (east - middle)
+            flux = flux + (face - pltpu.roll(face, 1, 1))
+            tendency = tendency + speed_ref[0, z + speed_at, pl.ds(speed_row, 8), :] * (east - west)
+            store(z, middle, tendency + (0.05 * time_step) * flux)
+            middle, base, below = upper, 2.0 + square, above
 
     def first(step, _):
-        z = step // first_chunks + 1
-        row = pl.multiple_of((step % first_chunks) * 8 + margin - 8, 8)
-        middle, tendency = rate(field, z, row, z - 1)
-        section[z - 1, pl.ds(row, 8), :] = middle + time_step * tendency
+        row = pl.multiple_of(step * 8 + margin - 8, 8)
+
+        def store(z, middle, change):
+            section[z - 1, pl.ds(row, 8), :] = middle + change
+
+        sweep(field, layers + 4, row, -1, store)
         return 0
 
-    lax.fori_loop(0, (layers + 2) * first_chunks, first, 0)
-    chunks = rows // 8
+    lax.fori_loop(0, rows // 8 + 2, first, 0)
 
     def second(step, _):
-        z = step // chunks
-        row = pl.multiple_of((step % chunks) * 8 + margin, 8)
-        middle, tendency = rate(section, z + 1, row, z + 1)
-        own = own_ref[z, pl.ds(row - margin, 8), :]
-        out_ref[z, pl.ds(row - margin, 8), :] = 0.5 * (own + middle + time_step * tendency)
+        row = pl.multiple_of(step * 8 + margin, 8)
+        out_row = pl.multiple_of(step * 8, 8)
+
+        def store(z, middle, change):
+            own = own_ref[z - 1, pl.ds(out_row, 8), :]
+            out_ref[z - 1, pl.ds(out_row, 8), :] = 0.5 * (own + middle + change)
+
+        sweep(section, layers + 2, row, 0, store)
         return 0
 
-    lax.fori_loop(0, layers * chunks, second, 0)
-
-
-def in_vmem(kernel, shape, count, scratch, flops):
+    lax.fori_loop(0, rows // 8, second, 0)
+
+
+def in_vmem(kernel, shapes, count, scratch, flops, mebibytes):
     spec = pl.BlockSpec(memory_space=pltpu.VMEM)
     return pl.pallas_call(
         kernel,
-        out_shape=jax.ShapeDtypeStruct(shape, jnp.float32),
+        out_shape=[jax.ShapeDtypeStruct(shape, jnp.float32) for shape in shapes],
         in_specs=[spec] * count,
-        out_specs=spec,
+        out_specs=[spec] * len(shapes),
         scratch_shapes=scratch,
-        compiler_params=pltpu.CompilerParams(vmem_limit_bytes=56 * 1024 * 1024),
+        compiler_params=pltpu.CompilerParams(vmem_limit_bytes=mebibytes * 1024 * 1024),
         cost_estimate=pl.CostEstimate(flops=flops, bytes_accessed=4 * 1024 * 1024, transcendentals=0),
     )
 
@@ -218,20 +238,23 @@
     modes_above = ring("gz", slabs, velocity_modes, -1)
     before = ring("wa", pencils, scalar[:, -2:], 1)
     after = ring("wa", pencils, scalar[:, :2], -1)
+    packed = (2 * fine_rows + 8, fine_x)
+    top, bottom = in_vmem(pack_kernel, (packed, packed), 3, [], 10, 16)(scalar, before, after)
+    below = ring("gz", slabs, top, 1)
+    above = ring("gz", slabs, bottom, -1)
 
     def to_rows(modes):
-        lines = jnp.einsum(
-            "nq,qdr->drn", modes.reshape(planes * kx, ky_count), synth_y, precision=lax.Precision.HIGH
-        )
+        lines = jnp.einsum("nq,qdr->drn", modes, synth_y, precision=lax.Precision.HIGH)
         return lax.all_to_all(lines, "wa", split_axis=0, concat_axis=0, tiled=True)
 
-    own = to_rows(velocity_modes)
-    half_done = in_vmem(
+    own = to_rows(velocity_modes.reshape(planes * kx, ky_count))
+    (half_done,) = in_vmem(
         functools.partial(stress_kernel, planes, kx),
-        (pencils, y_local, planes * kx),
+        ((pencils, y_local, planes * kx),),
         2,
         [pltpu.VMEM((y_local, kx_count), jnp.float32)],
         12 * planes * y_local * kx_count * padded_x,
+        32,
     )(own, synth_x)
     returned = lax.all_to_all(half_done, "wa", split_axis=0, concat_axis=0, tiled=True)
     stress = jnp.einsum("syn,qsy->nq", returned, analysis_y, precision=lax.Precision.HIGH)
@@ -242,31 +265,31 @@
     matrix_x = interp_matrix(numer_x // 8, (numer_x % 8).astype(jnp.float32) / 8.0, padded_x)
     synth_fine = jnp.dot(synth_x, matrix_x, precision=lax.Precision.HIGH)
 
-    top = jnp.concatenate([scalar[-2:], after[-2:], before[-2:]], axis=1)
-    bottom = jnp.concatenate([scalar[:2], after[:2], before[:2]], axis=1)
-    below = ring("gz", slabs, top, 1)
-    above = ring("gz", slabs, bottom, -1)
-
-    speed = in_vmem(
+    halo = to_rows(
+        jnp.concatenate([modes_below, modes_above]).reshape(2 * planes * kx, ky_count)
+    )
+    (speed,) = in_vmem(
         functools.partial(fine_kernel, layers, kx),
-        (2, fine_layers + 2, speed_rows, fine_x),
-        5,
+        ((2, fine_layers + 2, speed_rows, fine_x),),
+        4,
         [
             pltpu.VMEM((rows, kx_count), jnp.float32),
             pltpu.VMEM((layers + 4, speed_rows, kx_count), jnp.float32),
         ],
         12 * (fine_layers + 2) * speed_rows * kx_count * fine_x,
-    )(own, to_rows(modes_below), to_rows(modes_above), jnp.asarray(matrix_y), synth_fine)
-
-    scalar_next = in_vmem(
+        32,
+    )(own, halo, jnp.asarray(matrix_y), synth_fine)
+
+    (scalar_next,) = in_vmem(
         heun_kernel,
-        scalar.shape,
+        (scalar.shape,),
         6,
         [
             pltpu.VMEM((fine_layers + 4, fine_rows + 2 * margin, fine_x), jnp.float32),
             pltpu.VMEM((fine_layers + 2, fine_rows + 2 * margin, fine_x), jnp.float32),
         ],
         100 * fine_layers * fine_rows * fine_x,
+        32,
     )(scalar, before, after, below, above, speed)
     return (stress, scalar_next)
 

time: 131 us -> 136 us (1.038)
  waiting for transfers between devices: 25.3 us -> 64.7 us
  Pallas kernels: 45.7 us -> 28.6 us
  starting transfers between devices: 31.2 us -> 23.6 us
  local copies, waits for them, and re-layouts: 6.96 us -> 2.82 us
  matrix products: 16.2 us -> 13 us
  other arithmetic: 3.23 us -> 1.38 us
    ppermute x6, waiting for transfers between devices: 12 us -> 51.5 us  [ring(): lax.ppermute(value, axis, [(i, (i + step) % count) for i in range(count)])]
    pallas_call x3 -> x4, Pallas kernels: 45.7 us -> 28.6 us  [the longest x1 12.5 us: shards(): in_vmem(heun_kernel, (scalar.shape,), 6, [pltpu.VMEM((fine_layers + 4, fi...]
    ppermute x6, starting transfers between devices: 14.4 us -> 10.4 us  [ring(): lax.ppermute(value, axis, [(i, (i + step) % count) for i in range(count)])]
    ppermute x2 -> x0, local copies, waits for them, and re-layouts: 4.03 us -> none  [ring(): lax.ppermute(value, axis, [(i, (i + step) % count) for i in range(count)])]
    all_to_all x3 -> x2, waiting for transfers between devices: 13.3 us -> 9.39 us  [to_rows(): return lax.all_to_all(lines, 'wa', split_axis=0, concat_axis=0, tiled=True)]
    all_to_all x1, waiting for transfers between devices: 0.01 us -> 3.89 us  [shards(): lax.all_to_all(half_done, 'wa', split_axis=0, concat_axis=0, tiled=True)]
    all_to_all x3 -> x2, starting transfers between devices: 12.7 us -> 9.51 us  [to_rows(): return lax.all_to_all(lines, 'wa', split_axis=0, concat_axis=0, tiled=True)]
    dot_general x3 -> x2, matrix products: 8.1 us -> 6.24 us  [to_rows(): jnp.einsum('nq,qdr->drn', modes, synth_y, precision=lax.Precision.HIGH)]
  transfers between devices with their start and end apart: 10 -> 9, of which waited for: 3 -> 6; matrix products, arithmetic and copies ran while one was open for 19% -> 8% of each run, Pallas kernels for 35% -> 12%
where the time goes in v1:
time: 136 us; the launch traced here: 135 us
  waiting for transfers between devices  64.7 us (48%)
  Pallas kernels  28.6 us (21%)
  starting transfers between devices  23.6 us (17%)
  matrix products  13 us (10%)
  local copies, waits for them, and re-layouts  2.82 us (2%)
  between operations  1.4 us (1%)
  other arithmetic  1.38 us (1%)
    ppermute x6, waiting for transfers between devices, ring(): lax.ppermute(value, axis, [(i, (i + step) % count) for i in range(count)])  51.5 us
    pallas_call x1, Pallas kernels, shards(): in_vmem(heun_kernel, (scalar.shape,), 6, [pltpu.VMEM((fine_layers + 4, fi...  12.5 us
    ppermute x6, starting transfers between devices, ring(): lax.ppermute(value, axis, [(i, (i + step) % count) for i in range(count)])  10.4 us
    all_to_all x2, starting transfers between devices, to_rows(): return lax.all_to_all(lines, 'wa', split_axis=0, concat_axis=0, tiled=True)  9.51 us
    all_to_all x2, waiting for transfers between devices, to_rows(): return lax.all_to_all(lines, 'wa', split_axis=0, concat_axis=0, tiled=True)  9.39 us
    pallas_call x1, Pallas kernels, shards(): in_vmem(functools.partial(fine_kernel, layers, kx), ((2, fine_layers + 2,...  9.09 us
    dot_general x2, matrix products, to_rows(): jnp.einsum('nq,qdr->drn', modes, synth_y, precision=lax.Precision.HIGH)  6.24 us
    pallas_call x1, Pallas kernels, shards(): in_vmem(functools.partial(stress_kernel, planes, kx), ((pencils, y_local,...  5.47 us
  transfers between devices with their start and end apart: 9, of which 6 were waited for; matrix products, arithmetic and copies ran while one was open for 8% of the time, Pallas kernels for 12%

profile of v1, /device:TPU:0, one launch (start us, length us, event | category | flops | bytes accessed | tf_op | source)
XLA Modules:
  0.0 135.4 jit_solution(14494886267761782971)
XLA Ops:
  0.6 0.0 copy-start.11
  0.6 0.0 copy-start.3
  0.7 3.5 %fusion.39 = f32[8,104,256]{2,1,0:T(8,128)} fusion(f32[512,8,104]{0,2,1:T(8,128)} %constant.82, f32[256,512,1]{1,0,2:T(8,128)} %bitcast.22), kind=kOutput, calls=%fused_computation.64 | convolution fusion | flops 654311424 | bytes 3080192 | tf_op jit(solution)/shard_map/nq,qdr->drn/dot_general | solution.py:247
  4.1 5.2 %all-to-all-start = ((f32[8,104,256]{2,1,0:T(8,128)}), f32[8,104,256]{2,1,0:T(8,128)S(1)}, u32[]{:S(2)}, u32[]{:S(2)}) async-start(f32[8,104,256]{2,1,0:T(8,128)} %fusion.39), calls=%async_computation | async-start | bytes 1703936 | tf_op jit(solution)/shard_map/all_to_all | solution.py:248
  9.3 0.0 copy-done.11
  9.3 1.6 %collective-permute-start.4 = (f32[2,2,64,512]{3,2,1,0:T(8,128)S(1)}, f32[2,2,64,512]{3,2,1,0:T(8,128)}, u32[]{:S(2)}, u32[]{:S(2)}) collective-permute-start(f32[2,2,64,512]{3,2,1,0:T(8,128)S(1)} %copy-done.11), channel_id=1, source_target_pairs={{0,1},{1,2},{2,3},{3,0},{4,5},{5,6},{6,7},{7,4},{8,9},{9,10},{10,1... | collective-permute-start | bytes 1572872 | tf_op jit(solution)/shard_map/ppermute | solution.py:235
  11.0 2.2 %collective-permute-start.5 = (f32[2,2,64,512]{3,2,1,0:T(8,128)S(1)}, f32[2,2,64,512]{3,2,1,0:T(8,128)}, u32[]{:S(2)}, u32[]{:S(2)}) collective-permute-start(f32[2,2,64,512]{3,2,1,0:T(8,128)S(1)} %copy-done.11), channel_id=1, source_target_pairs={{0,3},{1,0},{2,1},{3,2},{4,7},{5,4},{6,5},{7,6},{8,11},{9,8},{10,9... | collective-permute-start | bytes 1572872 | tf_op jit(solution)/shard_map/ppermute | solution.py:235
  13.2 9.4 %all-to-all-done.block_ref.own_ref = f32[8,104,256]{2,1,0:T(8,128)S(1)} async-done(((f32[8,104,256]{2,1,0:T(8,128)}), f32[8,104,256]{2,1,0:T(8,128)S(1)}, u32[]{:S(2)}, u32[]{:S(2)}) %all-to-all-start) | async-done | bytes 852000 | tf_op jit(solution)/shard_map/all_to_all | solution.py:248
  22.6 0.0 copy-done.3
  22.6 5.5 %shard_map.86 = f32[8,96,256]{2,1,0:T(8,128)} custom-call(f32[8,104,256]{2,1,0:T(8,128)S(1)} %all-to-all-done.block_ref.own_ref, f32[512,768]{1,0:T(8,128)S(1)} %copy-done.3), custom_call_target="tpu_custom_call" | custom-call | flops 1811939328 | bytes 4194304 | tf_op jit(solution)/shard_map/pallas_call | solution.py:251
  28.1 0.0 copy-done.1
  28.1 0.0 copy-start.7
  28.1 3.7 %all-to-all-start.1 = ((f32[8,96,256]{2,1,0:T(8,128)}), f32[8,96,256]{2,1,0:T(8,128)S(1)}, u32[]{:S(2)}, u32[]{:S(2)}) async-start(f32[8,96,256]{2,1,0:T(8,128)} %shard_map.86), calls=%async_computation.1 | async-start | bytes 1572864 | tf_op jit(solution)/shard_map/all_to_all | solution.py:259
  31.8 0.0 collective-permute-done.4
  31.8 4.5 %collective-permute-done.5 = f32[2,2,64,512]{3,2,1,0:T(8,128)} collective-permute-done((f32[2,2,64,512]{3,2,1,0:T(8,128)S(1)}, f32[2,2,64,512]{3,2,1,0:T(8,128)}, u32[]{:S(2)}, u32[]{:S(2)}) %collective-permute-start.5) | collective-permute-done | bytes 524320 | tf_op jit(solution)/shard_map/ppermute | solution.py:235
  36.3 1.3 pad_maximum_fusion
  37.6 0.0 copy-done.7
  37.6 2.8 %fusion.40 = f32[8,104,512]{2,1,0:T(8,128)} fusion(f32[512,8,104]{0,2,1:T(8,128)S(1)} %copy-done.7, f32[512,512,1]{1,0,2:T(8,128)S(1)} %bitcast.21), kind=kOutput, calls=%fused_computation.65 | convolution fusion | flops 1308622848 | bytes 4456448 | tf_op jit(solution)/shard_map/nq,qdr->drn/dot_general | solution.py:247
  40.4 0.0 copy-start
  40.4 3.9 %all-to-all-done.1 = f32[8,96,256]{2,1,0:T(8,128)S(1)} async-done(((f32[8,96,256]{2,1,0:T(8,128)}), f32[8,96,256]{2,1,0:T(8,128)S(1)}, u32[]{:S(2)}, u32[]{:S(2)}) %all-to-all-start.1) | async-done | bytes 786464 | tf_op jit(solution)/shard_map/all_to_all | solution.py:259
  44.3 0.0 copy-start.8
  44.3 4.3 %all-to-all-start.2 = ((f32[8,104,512]{2,1,0:T(8,128)}), f32[8,104,512]{2,1,0:T(8,128)}, u32[]{:S(2)}, u32[]{:S(2)}) async-start(f32[8,104,512]{2,1,0:T(8,128)} %fusion.40), calls=%async_computation.2 | async-start | bytes 3407872 | tf_op jit(solution)/shard_map/all_to_all | solution.py:248
  48.6 0.0 copy-done
  48.6 0.0 copy-start.4
  48.6 0.0 copy-done.8
  48.7 0.4 collective-permute-start
  49.1 2.3 %collective-permute-start.1 = (f32[4,2,1024]{2,1,0:T(2,128)S(1)}, f32[4,2,1024]{2,1,0:T(2,128)S(1)}, u32[]{:S(2)}, u32[]{:S(2)}) collective-permute-start(f32[4,2,1024]{2,1,0:T(2,128)S(1)} %get-tuple-element.6), channel_id=1, source_target_pairs={{0,28},{4,0},{8,4},{12,8},{16,12},{20,16},{24,20},{28,24},{1,29},{... | collective-permute-start | bytes 98312 | tf_op jit(solution)/shard_map/ppermute | solution.py:235
  52.1 18.9 %collective-permute-done.before_ref = f32[4,2,1024]{2,1,0:T(2,128)S(1)} collective-permute-done((f32[4,2,1024]{2,1,0:T(2,128)S(1)}, f32[4,2,1024]{2,1,0:T(2,128)S(1)}, u32[]{:S(2)}, u32[]{:S(2)}) %collective-permute-start) | collective-permute-done | bytes 32800 | tf_op jit(solution)/shard_map/ppermute | solution.py:235
  71.0 0.0 collective-permute-done.1.after_ref
  71.0 1.5 %shard_map.87 = (f32[264,1024]{1,0:T(8,128)}, f32[264,1024]{1,0:T(8,128)}) custom-call(f32[4,128,1024]{2,1,0:T(8,128)S(1)} %copy-done, f32[4,2,1024]{2,1,0:T(2,128)S(1)} %collective-permute-done.before_ref, f32[4,2,1024]{2,1,0:T(2,128)S(1)} %collective-permute-done.1.after_ref), custom_call_target="tpu_custom_call" | custom-call | flops 10 | bytes 4194304 | tf_op jit(solution)/shard_map/pallas_call | solution.py:242
  72.6 1.6 %collective-permute-start.2 = (f32[264,1024]{1,0:T(8,128)}, f32[264,1024]{1,0:T(8,128)S(1)}, u32[]{:S(2)}, u32[]{:S(2)}) collective-permute-start(f32[264,1024]{1,0:T(8,128)} %get-tuple-element.4), channel_id=1, source_target_pairs={{0,1},{1,2},{2,3},{3,0},{4,5},{5,6},{6,7},{7,4},{8,9},{9,10},{10,1... | collective-permute-start | bytes 3244040 | tf_op jit(solution)/shard_map/ppermute | solution.py:235
  74.1 2.3 %collective-permute-start.3 = (f32[264,1024]{1,0:T(8,128)}, f32[264,1024]{1,0:T(8,128)}, u32[]{:S(2)}, u32[]{:S(2)}) collective-permute-start(f32[264,1024]{1,0:T(8,128)} %get-tuple-element.5), channel_id=1, source_target_pairs={{0,3},{1,0},{2,1},{3,2},{4,7},{5,4},{6,5},{7,6},{8,11},{9,8},{10,9... | collective-permute-start | bytes 3244040 | tf_op jit(solution)/shard_map/ppermute | solution.py:235
  76.4 0.0 copy-done.4
  76.4 0.0 copy-start.9
  76.4 0.0 copy-start.10
  76.4 5.1 %fusion.synth_ref = f32[512,1024]{1,0:T(8,128)} fusion(f32[512,768]{1,0:T(8,128)S(1)} %copy-done.4, f32[1024]{0:T(1024)S(1)} %get-tuple-element.15, s32[1024]{0:T(1024)S(1)} %get-tuple-element.8, f32[1024]{0:T(1024)S(1)} %get-tuple-element.14, s32[1024]{0:T(1024)S(1)} %get-tuple-element.9, f32[1024]{0:T(1024)S(1)} %get-tuple-element.13, ...), kind=kOutput, calls=%fused_computation | convolution fusion | flops 2424569856 | bytes 3702784 | tf_op jit(solution)/shard_map/dot_general | solution.py:266
  81.5 0.0 copy-done.9
  81.5 0.0 copy-done.10
  81.5 0.0 copy-start.5
  81.5 1.6 %fusion.18 = bf16[256,512]{1,0:T(8,128)(2,1)} fusion(f32[8,96,256]{2,1,0:T(8,128)S(1)} %copy-done.9, f32[512,8,96]{0,2,1:T(8,128)S(1)} %copy-done.10), kind=kOutput, calls=%fused_computation.23 | convolution fusion | flops 604241920 | bytes 2621440 | tf_op jit(solution)/shard_map/syn,qsy->nq/dot_general | solution.py:260
  83.1 0.0 all-to-all-done.2.halo_ref
  83.1 0.0 copy-done.5
  83.1 1.2 copy-done.2
  84.3 1.6 %copy-done.6 = f32[512,1024]{1,0:T(8,128)S(1)} copy-done((f32[512,1024]{1,0:T(8,128)S(1)}, f32[512,1024]{1,0:T(8,128)}, u32[]{:S(2)}) %copy-start.6) | copy-done | bytes 2097176
  85.9 9.1 %shard_map.88.speed_ref = f32[2,6,144,1024]{3,2,1,0:T(8,128)S(1)} custom-call(f32[8,104,256]{2,1,0:T(8,128)S(1)} %copy-done.2, f32[8,104,512]{2,1,0:T(8,128)} %all-to-all-done.2.halo_ref, f32[144,104]{1,0:T(8,128)S(1)} %copy-done.5, f32[512,1024]{1,0:T(8,128)S(1)} %copy-done.6), custom_call_target="tpu_custom_call" | custom-call | flops 5435817984 | bytes 4194304 | tf_op jit(solution)/shard_map/pallas_call | solution.py:271
  95.0 6.4 %collective-permute-done.2.below_ref = f32[264,1024]{1,0:T(8,128)S(1)} collective-permute-done((f32[264,1024]{1,0:T(8,128)}, f32[264,1024]{1,0:T(8,128)S(1)}, u32[]{:S(2)}, u32[]{:S(2)}) %collective-permute-start.2) | collective-permute-done | bytes 1081376 | tf_op jit(solution)/shard_map/ppermute | solution.py:235
  101.3 21.6 %collective-permute-done.3.above_ref = f32[264,1024]{1,0:T(8,128)} collective-permute-done((f32[264,1024]{1,0:T(8,128)}, f32[264,1024]{1,0:T(8,128)}, u32[]{:S(2)}, u32[]{:S(2)}) %collective-permute-start.3) | collective-permute-done | bytes 1081376 | tf_op jit(solution)/shard_map/ppermute | solution.py:235
  123.0 12.5 %shard_map.89 = f32[4,128,1024]{2,1,0:T(8,128)} custom-call(f32[4,128,1024]{2,1,0:T(8,128)S(1)} %copy-done, f32[4,2,1024]{2,1,0:T(2,128)S(1)} %collective-permute-done.before_ref, f32[4,2,1024]{2,1,0:T(2,128)S(1)} %collective-permute-done.1.after_ref, f32[264,1024]{1,0:T(8,128)S(1)} %collective-permute-done.2.below_ref, ...), custom_call_target="tpu_custom_call" | custom-call | flops 52428800 | bytes 4194304 | tf_op jit(solution)/shard_map/pallas_call | solution.py:283
  (8 shorter events, 0.1 us)
Async XLA Ops:
  0.6 8.7 %copy-start.11 = (f32[2,2,64,512]{3,2,1,0:T(8,128)S(1)}, f32[2,2,64,512]{3,2,1,0:T(8,128)}, u32[]{:S(2)}) copy-start(f32[2,2,64,512]{3,2,1,0:T(8,128)} %param.7) | copy-start | bytes 1572868
  0.6 22.0 %copy-start.3 = (f32[512,768]{1,0:T(8,128)S(1)}, f32[512,768]{1,0:T(8,128)}, u32[]{:S(2)}) copy-start(f32[512,768]{1,0:T(8,128)} %constant.79.clone.table_ref) | copy-start | bytes 4718596
  4.1 18.5 %all-to-all-start = ((f32[8,104,256]{2,1,0:T(8,128)}), f32[8,104,256]{2,1,0:T(8,128)S(1)}, u32[]{:S(2)}, u32[]{:S(2)}) async-start(f32[8,104,256]{2,1,0:T(8,128)} %fusion.39), calls=%async_computation | async-start | bytes 1703936 | tf_op jit(solution)/shard_map/all_to_all | solution.py:248
  9.3 22.4 %collective-permute-start.4 = (f32[2,2,64,512]{3,2,1,0:T(8,128)S(1)}, f32[2,2,64,512]{3,2,1,0:T(8,128)}, u32[]{:S(2)}, u32[]{:S(2)}) collective-permute-start(f32[2,2,64,512]{3,2,1,0:T(8,128)S(1)} %copy-done.11), channel_id=1, source_target_pairs={{0,1},{1,2},{2,3},{3,0},{4,5},{5,6},{6,7},{7,4},{8,9},{9,10},{10,1... | collective-permute-start | bytes 1572872 | tf_op jit(solution)/shard_map/ppermute | solution.py:235
  11.0 25.3 %collective-permute-start.5 = (f32[2,2,64,512]{3,2,1,0:T(8,128)S(1)}, f32[2,2,64,512]{3,2,1,0:T(8,128)}, u32[]{:S(2)}, u32[]{:S(2)}) collective-permute-start(f32[2,2,64,512]{3,2,1,0:T(8,128)S(1)} %copy-done.11), channel_id=1, source_target_pairs={{0,3},{1,0},{2,1},{3,2},{4,7},{5,4},{6,5},{7,6},{8,11},{9,8},{10,9... | collective-permute-start | bytes 1572872 | tf_op jit(solution)/shard_map/ppermute | solution.py:235
  22.6 5.5 %copy-start.1 = (f32[8,104,256]{2,1,0:T(8,128)}, f32[8,104,256]{2,1,0:T(8,128)S(1)}, u32[]{:S(2)}) copy-start(f32[8,104,256]{2,1,0:T(8,128)S(1)} %all-to-all-done.block_ref.own_ref) | copy-start | bytes 2555908
  28.1 9.5 %copy-start.7 = (f32[512,8,104]{0,2,1:T(8,128)S(1)}, f32[512,8,104]{0,2,1:T(8,128)}, u32[]{:S(2)}) copy-start(f32[512,8,104]{0,2,1:T(8,128)} %constant.82) | copy-start | bytes 5111812
  28.1 16.2 %all-to-all-start.1 = ((f32[8,96,256]{2,1,0:T(8,128)}), f32[8,96,256]{2,1,0:T(8,128)S(1)}, u32[]{:S(2)}, u32[]{:S(2)}) async-start(f32[8,96,256]{2,1,0:T(8,128)} %shard_map.86), calls=%async_computation.1 | async-start | bytes 1572864 | tf_op jit(solution)/shard_map/all_to_all | solution.py:259
  40.4 8.2 %copy-start = (f32[4,128,1024]{2,1,0:T(8,128)S(1)}, f32[4,128,1024]{2,1,0:T(8,128)}, u32[]{:S(2)}) copy-start(f32[4,128,1024]{2,1,0:T(8,128)} %own_ref.1) | copy-start | bytes 6291460
  44.3 4.4 %copy-start.8 = (f32[8,96,256]{2,1,0:T(8,128)}, f32[8,96,256]{2,1,0:T(8,128)S(1)}, u32[]{:S(2)}) copy-start(f32[8,96,256]{2,1,0:T(8,128)S(1)} %all-to-all-done.1) | copy-start | bytes 2359300
  44.3 38.8 %all-to-all-start.2 = ((f32[8,104,512]{2,1,0:T(8,128)}), f32[8,104,512]{2,1,0:T(8,128)}, u32[]{:S(2)}, u32[]{:S(2)}) async-start(f32[8,104,512]{2,1,0:T(8,128)} %fusion.40), calls=%async_computation.2 | async-start | bytes 3407872 | tf_op jit(solution)/shard_map/all_to_all | solution.py:248
  48.6 27.8 %copy-start.4 = (f32[512,768]{1,0:T(8,128)S(1)}, f32[512,768]{1,0:T(8,128)}, u32[]{:S(2)}) copy-start(f32[512,768]{1,0:T(8,128)} %constant.79.clone.table_ref) | copy-start | bytes 4718596
  48.7 22.4 %collective-permute-start = (f32[4,2,1024]{2,1,0:T(2,128)S(1)}, f32[4,2,1024]{2,1,0:T(2,128)S(1)}, u32[]{:S(2)}, u32[]{:S(2)}) collective-permute-start(f32[4,2,1024]{2,1,0:T(2,128)S(1)} %get-tuple-element.7), channel_id=1, source_target_pairs={{0,4},{4,8},{8,12},{12,16},{16,20},{20,24},{24,28},{28,0},{1,5},{5... | collective-permute-start | bytes 98312 | tf_op jit(solution)/shard_map/ppermute | solution.py:235
  49.1 22.0 %collective-permute-start.1 = (f32[4,2,1024]{2,1,0:T(2,128)S(1)}, f32[4,2,1024]{2,1,0:T(2,128)S(1)}, u32[]{:S(2)}, u32[]{:S(2)}) collective-permute-start(f32[4,2,1024]{2,1,0:T(2,128)S(1)} %get-tuple-element.6), channel_id=1, source_target_pairs={{0,28},{4,0},{8,4},{12,8},{16,12},{20,16},{24,20},{28,24},{1,29},{... | collective-permute-start | bytes 98312 | tf_op jit(solution)/shard_map/ppermute | solution.py:235
  72.6 28.8 %collective-permute-start.2 = (f32[264,1024]{1,0:T(8,128)}, f32[264,1024]{1,0:T(8,128)S(1)}, u32[]{:S(2)}, u32[]{:S(2)}) collective-permute-start(f32[264,1024]{1,0:T(8,128)} %get-tuple-element.4), channel_id=1, source_target_pairs={{0,1},{1,2},{2,3},{3,0},{4,5},{5,6},{6,7},{7,4},{8,9},{9,10},{10,1... | collective-permute-start | bytes 3244040 | tf_op jit(solution)/shard_map/ppermute | solution.py:235
  74.1 48.8 %collective-permute-start.3 = (f32[264,1024]{1,0:T(8,128)}, f32[264,1024]{1,0:T(8,128)}, u32[]{:S(2)}, u32[]{:S(2)}) collective-permute-start(f32[264,1024]{1,0:T(8,128)} %get-tuple-element.5), channel_id=1, source_target_pairs={{0,3},{1,0},{2,1},{3,2},{4,7},{5,4},{6,5},{7,6},{8,11},{9,8},{10,9... | collective-permute-start | bytes 3244040 | tf_op jit(solution)/shard_map/ppermute | solution.py:235
  76.4 5.1 %copy-start.9 = (f32[8,96,256]{2,1,0:T(8,128)S(1)}, f32[8,96,256]{2,1,0:T(8,128)}, u32[]{:S(2)}) copy-start(f32[8,96,256]{2,1,0:T(8,128)} %copy-done.8) | copy-start | bytes 2359300
  76.4 5.1 %copy-start.10 = (f32[512,8,96]{0,2,1:T(8,128)S(1)}, f32[512,8,96]{0,2,1:T(8,128)}, u32[]{:S(2)}) copy-start(f32[512,8,96]{0,2,1:T(8,128)} %constant.83) | copy-start | bytes 4718596
  81.5 1.6 %copy-start.5 = (f32[144,104]{1,0:T(8,128)S(1)}, f32[144,104]{1,0:T(8,128)}, u32[]{:S(2)}) copy-start(f32[144,104]{1,0:T(8,128)} %constant.80.clone.matrix_y_ref) | copy-start | bytes 179716
  83.1 1.2 copy-start.2
  84.3 1.6 %copy-start.6 = (f32[512,1024]{1,0:T(8,128)S(1)}, f32[512,1024]{1,0:T(8,128)}, u32[]{:S(2)}) copy-start(f32[512,1024]{1,0:T(8,128)} %fusion.synth_ref) | copy-start | bytes 6291460

commit v2 on v1

--- a/solution.py
+++ b/solution.py
@@ -172,7 +172,7 @@
         sweep(field, layers + 4, row, -1, store)
         return 0
 
-    lax.fori_loop(0, rows // 8 + 2, first, 0)
+    lax.fori_loop(0, rows // 8 + 2, first, 0, unroll=2)
 
     def second(step, _):
         row = pl.multiple_of(step * 8 + margin, 8)
@@ -185,7 +185,7 @@
         sweep(section, layers + 2, row, 0, store)
         return 0
 
-    lax.fori_loop(0, rows // 8, second, 0)
+    lax.fori_loop(0, rows // 8, second, 0, unroll=2)
 
 
 def in_vmem(kernel, shapes, count, scratch, flops, mebibytes):
@@ -265,9 +265,7 @@
     matrix_x = interp_matrix(numer_x // 8, (numer_x % 8).astype(jnp.float32) / 8.0, padded_x)
     synth_fine = jnp.dot(synth_x, matrix_x, precision=lax.Precision.HIGH)
 
-    halo = to_rows(
-        jnp.concatenate([modes_below, modes_above]).reshape(2 * planes * kx, ky_count)
-    )
+    halo = to_rows(jnp.concatenate([modes_below, modes_above]).reshape(2 * planes * kx, ky_count))
     (speed,) = in_vmem(
         functools.partial(fine_kernel, layers, kx),
         ((2, fine_layers + 2, speed_rows, fine_x),),

time: 136 us -> 138 us (1.015)
  Pallas kernels: 28.6 us -> 30.2 us
    pallas_call x1, Pallas kernels: 12.5 us -> 14.1 us  [shards(): in_vmem(heun_kernel, (scalar.shape,), 6, [pltpu.VMEM((fine_layers + 4, fi...]
where the time goes in v2:
time: 138 us; the launch traced here: 137 us
  waiting for transfers between devices  64.7 us (47%)
  Pallas kernels  30.2 us (22%)
  starting transfers between devices  23.6 us (17%)
  matrix products  13 us (9%)
  local copies, waits for them, and re-layouts  2.82 us (2%)
  between operations  1.4 us (1%)
    ppermute x6, waiting for transfers between devices, ring(): lax.ppermute(value, axis, [(i, (i + step) % count) for i in range(count)])  51.5 us
    pallas_call x1, Pallas kernels, shards(): in_vmem(heun_kernel, (scalar.shape,), 6, [pltpu.VMEM((fine_layers + 4, fi...  14.1 us
    ppermute x6, starting transfers between devices, ring(): lax.ppermute(value, axis, [(i, (i + step) % count) for i in range(count)])  10.4 us
    all_to_all x2, starting transfers between devices, to_rows(): return lax.all_to_all(lines, 'wa', split_axis=0, concat_axis=0, tiled=True)  9.51 us
    all_to_all x2, waiting for transfers between devices, to_rows(): return lax.all_to_all(lines, 'wa', split_axis=0, concat_axis=0, tiled=True)  9.39 us
    pallas_call x1, Pallas kernels, shards(): in_vmem(functools.partial(fine_kernel, layers, kx), ((2, fine_layers + 2,...  9.09 us
    dot_general x2, matrix products, to_rows(): jnp.einsum('nq,qdr->drn', modes, synth_y, precision=lax.Precision.HIGH)  6.24 us
    pallas_call x1, Pallas kernels, shards(): in_vmem(functools.partial(stress_kernel, planes, kx), ((pencils, y_local,...  5.47 us
  transfers between devices with their start and end apart: 9, of which 6 were waited for; matrix products, arithmetic and copies ran while one was open for 8% of the time, Pallas kernels for 12%

profile of v2, /device:TPU:0, one launch (start us, length us, event | category | flops | bytes accessed | tf_op | source)
XLA Modules:
  0.0 137.1 jit_solution(9991897788295974252)
XLA Ops:
  0.6 0.0 copy-start.11
  0.6 0.0 copy-start.3
  0.7 3.5 %fusion.39 = f32[8,104,256]{2,1,0:T(8,128)} fusion(f32[512,8,104]{0,2,1:T(8,128)} %constant.82, f32[256,512,1]{1,0,2:T(8,128)} %bitcast.22), kind=kOutput, calls=%fused_computation.64 | convolution fusion | flops 654311424 | bytes 3080192 | tf_op jit(solution)/shard_map/nq,qdr->drn/dot_general | solution.py:247
  4.1 5.2 %all-to-all-start = ((f32[8,104,256]{2,1,0:T(8,128)}), f32[8,104,256]{2,1,0:T(8,128)S(1)}, u32[]{:S(2)}, u32[]{:S(2)}) async-start(f32[8,104,256]{2,1,0:T(8,128)} %fusion.39), calls=%async_computation | async-start | bytes 1703936 | tf_op jit(solution)/shard_map/all_to_all | solution.py:248
  9.3 0.0 copy-done.11
  9.3 1.6 %collective-permute-start.4 = (f32[2,2,64,512]{3,2,1,0:T(8,128)S(1)}, f32[2,2,64,512]{3,2,1,0:T(8,128)}, u32[]{:S(2)}, u32[]{:S(2)}) collective-permute-start(f32[2,2,64,512]{3,2,1,0:T(8,128)S(1)} %copy-done.11), channel_id=1, source_target_pairs={{0,1},{1,2},{2,3},{3,0},{4,5},{5,6},{6,7},{7,4},{8,9},{9,10},{10,1... | collective-permute-start | bytes 1572872 | tf_op jit(solution)/shard_map/ppermute | solution.py:235
  11.0 2.2 %collective-permute-start.5 = (f32[2,2,64,512]{3,2,1,0:T(8,128)S(1)}, f32[2,2,64,512]{3,2,1,0:T(8,128)}, u32[]{:S(2)}, u32[]{:S(2)}) collective-permute-start(f32[2,2,64,512]{3,2,1,0:T(8,128)S(1)} %copy-done.11), channel_id=1, source_target_pairs={{0,3},{1,0},{2,1},{3,2},{4,7},{5,4},{6,5},{7,6},{8,11},{9,8},{10,9... | collective-permute-start | bytes 1572872 | tf_op jit(solution)/shard_map/ppermute | solution.py:235
  13.2 9.4 %all-to-all-done.block_ref.own_ref = f32[8,104,256]{2,1,0:T(8,128)S(1)} async-done(((f32[8,104,256]{2,1,0:T(8,128)}), f32[8,104,256]{2,1,0:T(8,128)S(1)}, u32[]{:S(2)}, u32[]{:S(2)}) %all-to-all-start) | async-done | bytes 852000 | tf_op jit(solution)/shard_map/all_to_all | solution.py:248
  22.6 0.0 copy-done.3
  22.6 5.5 %shard_map.86 = f32[8,96,256]{2,1,0:T(8,128)} custom-call(f32[8,104,256]{2,1,0:T(8,128)S(1)} %all-to-all-done.block_ref.own_ref, f32[512,768]{1,0:T(8,128)S(1)} %copy-done.3), custom_call_target="tpu_custom_call" | custom-call | flops 1811939328 | bytes 4194304 | tf_op jit(solution)/shard_map/pallas_call | solution.py:251
  28.1 0.0 copy-done.1
  28.1 0.0 copy-start.7
  28.1 3.7 %all-to-all-start.1 = ((f32[8,96,256]{2,1,0:T(8,128)}), f32[8,96,256]{2,1,0:T(8,128)S(1)}, u32[]{:S(2)}, u32[]{:S(2)}) async-start(f32[8,96,256]{2,1,0:T(8,128)} %shard_map.86), calls=%async_computation.1 | async-start | bytes 1572864 | tf_op jit(solution)/shard_map/all_to_all | solution.py:259
  31.8 0.0 collective-permute-done.4
  31.8 4.5 %collective-permute-done.5 = f32[2,2,64,512]{3,2,1,0:T(8,128)} collective-permute-done((f32[2,2,64,512]{3,2,1,0:T(8,128)S(1)}, f32[2,2,64,512]{3,2,1,0:T(8,128)}, u32[]{:S(2)}, u32[]{:S(2)}) %collective-permute-start.5) | collective-permute-done | bytes 524320 | tf_op jit(solution)/shard_map/ppermute | solution.py:235
  36.3 1.3 pad_maximum_fusion
  37.6 0.0 copy-done.7
  37.6 2.8 %fusion.40 = f32[8,104,512]{2,1,0:T(8,128)} fusion(f32[512,8,104]{0,2,1:T(8,128)S(1)} %copy-done.7, f32[512,512,1]{1,0,2:T(8,128)S(1)} %bitcast.21), kind=kOutput, calls=%fused_computation.65 | convolution fusion | flops 1308622848 | bytes 4456448 | tf_op jit(solution)/shard_map/nq,qdr->drn/dot_general | solution.py:247
  40.4 0.0 copy-start
  40.4 3.9 %all-to-all-done.1 = f32[8,96,256]{2,1,0:T(8,128)S(1)} async-done(((f32[8,96,256]{2,1,0:T(8,128)}), f32[8,96,256]{2,1,0:T(8,128)S(1)}, u32[]{:S(2)}, u32[]{:S(2)}) %all-to-all-start.1) | async-done | bytes 786464 | tf_op jit(solution)/shard_map/all_to_all | solution.py:259
  44.3 0.0 copy-start.8
  44.3 4.3 %all-to-all-start.2 = ((f32[8,104,512]{2,1,0:T(8,128)}), f32[8,104,512]{2,1,0:T(8,128)}, u32[]{:S(2)}, u32[]{:S(2)}) async-start(f32[8,104,512]{2,1,0:T(8,128)} %fusion.40), calls=%async_computation.2 | async-start | bytes 3407872 | tf_op jit(solution)/shard_map/all_to_all | solution.py:248
  48.6 0.0 copy-done
  48.6 0.0 copy-start.4
  48.6 0.0 copy-done.8
  48.7 0.4 collective-permute-start
  49.1 2.3 %collective-permute-start.1 = (f32[4,2,1024]{2,1,0:T(2,128)S(1)}, f32[4,2,1024]{2,1,0:T(2,128)S(1)}, u32[]{:S(2)}, u32[]{:S(2)}) collective-permute-start(f32[4,2,1024]{2,1,0:T(2,128)S(1)} %get-tuple-element.6), channel_id=1, source_target_pairs={{0,28},{4,0},{8,4},{12,8},{16,12},{20,16},{24,20},{28,24},{1,29},{... | collective-permute-start | bytes 98312 | tf_op jit(solution)/shard_map/ppermute | solution.py:235
  52.1 18.9 %collective-permute-done.before_ref = f32[4,2,1024]{2,1,0:T(2,128)S(1)} collective-permute-done((f32[4,2,1024]{2,1,0:T(2,128)S(1)}, f32[4,2,1024]{2,1,0:T(2,128)S(1)}, u32[]{:S(2)}, u32[]{:S(2)}) %collective-permute-start) | collective-permute-done | bytes 32800 | tf_op jit(solution)/shard_map/ppermute | solution.py:235
  71.0 0.0 collective-permute-done.1.after_ref
  71.0 1.5 %shard_map.87 = (f32[264,1024]{1,0:T(8,128)}, f32[264,1024]{1,0:T(8,128)}) custom-call(f32[4,128,1024]{2,1,0:T(8,128)S(1)} %copy-done, f32[4,2,1024]{2,1,0:T(2,128)S(1)} %collective-permute-done.before_ref, f32[4,2,1024]{2,1,0:T(2,128)S(1)} %collective-permute-done.1.after_ref), custom_call_target="tpu_custom_call" | custom-call | flops 10 | bytes 4194304 | tf_op jit(solution)/shard_map/pallas_call | solution.py:242
  72.6 1.6 %collective-permute-start.2 = (f32[264,1024]{1,0:T(8,128)}, f32[264,1024]{1,0:T(8,128)S(1)}, u32[]{:S(2)}, u32[]{:S(2)}) collective-permute-start(f32[264,1024]{1,0:T(8,128)} %get-tuple-element.4), channel_id=1, source_target_pairs={{0,1},{1,2},{2,3},{3,0},{4,5},{5,6},{6,7},{7,4},{8,9},{9,10},{10,1... | collective-permute-start | bytes 3244040 | tf_op jit(solution)/shard_map/ppermute | solution.py:235
  74.1 2.3 %collective-permute-start.3 = (f32[264,1024]{1,0:T(8,128)}, f32[264,1024]{1,0:T(8,128)}, u32[]{:S(2)}, u32[]{:S(2)}) collective-permute-start(f32[264,1024]{1,0:T(8,128)} %get-tuple-element.5), channel_id=1, source_target_pairs={{0,3},{1,0},{2,1},{3,2},{4,7},{5,4},{6,5},{7,6},{8,11},{9,8},{10,9... | collective-permute-start | bytes 3244040 | tf_op jit(solution)/shard_map/ppermute | solution.py:235
  76.4 0.0 copy-done.4
  76.4 0.0 copy-start.9
  76.4 0.0 copy-start.10
  76.4 5.1 %fusion.synth_ref = f32[512,1024]{1,0:T(8,128)} fusion(f32[512,768]{1,0:T(8,128)S(1)} %copy-done.4, f32[1024]{0:T(1024)S(1)} %get-tuple-element.15, s32[1024]{0:T(1024)S(1)} %get-tuple-element.8, f32[1024]{0:T(1024)S(1)} %get-tuple-element.14, s32[1024]{0:T(1024)S(1)} %get-tuple-element.9, f32[1024]{0:T(1024)S(1)} %get-tuple-element.13, ...), kind=kOutput, calls=%fused_computation | convolution fusion | flops 2424569856 | bytes 3702784 | tf_op jit(solution)/shard_map/dot_general | solution.py:266
  81.5 0.0 copy-done.9
  81.5 0.0 copy-done.10
  81.5 0.0 copy-start.5
  81.5 1.6 %fusion.18 = bf16[256,512]{1,0:T(8,128)(2,1)} fusion(f32[8,96,256]{2,1,0:T(8,128)S(1)} %copy-done.9, f32[512,8,96]{0,2,1:T(8,128)S(1)} %copy-done.10), kind=kOutput, calls=%fused_computation.23 | convolution fusion | flops 604241920 | bytes 2621440 | tf_op jit(solution)/shard_map/syn,qsy->nq/dot_general | solution.py:260
  83.1 0.0 all-to-all-done.2.halo_ref
  83.1 0.0 copy-done.5
  83.1 1.2 copy-done.2
  84.3 1.6 %copy-done.6 = f32[512,1024]{1,0:T(8,128)S(1)} copy-done((f32[512,1024]{1,0:T(8,128)S(1)}, f32[512,1024]{1,0:T(8,128)}, u32[]{:S(2)}) %copy-start.6) | copy-done | bytes 2097176
  85.9 9.1 %shard_map.88.speed_ref = f32[2,6,144,1024]{3,2,1,0:T(8,128)S(1)} custom-call(f32[8,104,256]{2,1,0:T(8,128)S(1)} %copy-done.2, f32[8,104,512]{2,1,0:T(8,128)} %all-to-all-done.2.halo_ref, f32[144,104]{1,0:T(8,128)S(1)} %copy-done.5, f32[512,1024]{1,0:T(8,128)S(1)} %copy-done.6), custom_call_target="tpu_custom_call" | custom-call | flops 5435817984 | bytes 4194304 | tf_op jit(solution)/shard_map/pallas_call | solution.py:269
  95.0 6.4 %collective-permute-done.2.below_ref = f32[264,1024]{1,0:T(8,128)S(1)} collective-permute-done((f32[264,1024]{1,0:T(8,128)}, f32[264,1024]{1,0:T(8,128)S(1)}, u32[]{:S(2)}, u32[]{:S(2)}) %collective-permute-start.2) | collective-permute-done | bytes 1081376 | tf_op jit(solution)/shard_map/ppermute | solution.py:235
  101.3 21.6 %collective-permute-done.3.above_ref = f32[264,1024]{1,0:T(8,128)} collective-permute-done((f32[264,1024]{1,0:T(8,128)}, f32[264,1024]{1,0:T(8,128)}, u32[]{:S(2)}, u32[]{:S(2)}) %collective-permute-start.3) | collective-permute-done | bytes 1081376 | tf_op jit(solution)/shard_map/ppermute | solution.py:235
  123.0 14.1 %shard_map.89 = f32[4,128,1024]{2,1,0:T(8,128)} custom-call(f32[4,128,1024]{2,1,0:T(8,128)S(1)} %copy-done, f32[4,2,1024]{2,1,0:T(2,128)S(1)} %collective-permute-done.before_ref, f32[4,2,1024]{2,1,0:T(2,128)S(1)} %collective-permute-done.1.after_ref, f32[264,1024]{1,0:T(8,128)S(1)} %collective-permute-done.2.below_ref, ...), custom_call_target="tpu_custom_call" | custom-call | flops 52428800 | bytes 4194304 | tf_op jit(solution)/shard_map/pallas_call | solution.py:281
  (8 shorter events, 0.1 us)
Async XLA Ops:
  0.6 8.7 %copy-start.11 = (f32[2,2,64,512]{3,2,1,0:T(8,128)S(1)}, f32[2,2,64,512]{3,2,1,0:T(8,128)}, u32[]{:S(2)}) copy-start(f32[2,2,64,512]{3,2,1,0:T(8,128)} %param.7) | copy-start | bytes 1572868
  0.6 22.0 %copy-start.3 = (f32[512,768]{1,0:T(8,128)S(1)}, f32[512,768]{1,0:T(8,128)}, u32[]{:S(2)}) copy-start(f32[512,768]{1,0:T(8,128)} %constant.79.clone.table_ref) | copy-start | bytes 4718596
  4.1 18.5 %all-to-all-start = ((f32[8,104,256]{2,1,0:T(8,128)}), f32[8,104,256]{2,1,0:T(8,128)S(1)}, u32[]{:S(2)}, u32[]{:S(2)}) async-start(f32[8,104,256]{2,1,0:T(8,128)} %fusion.39), calls=%async_computation | async-start | bytes 1703936 | tf_op jit(solution)/shard_map/all_to_all | solution.py:248
  9.3 22.4 %collective-permute-start.4 = (f32[2,2,64,512]{3,2,1,0:T(8,128)S(1)}, f32[2,2,64,512]{3,2,1,0:T(8,128)}, u32[]{:S(2)}, u32[]{:S(2)}) collective-permute-start(f32[2,2,64,512]{3,2,1,0:T(8,128)S(1)} %copy-done.11), channel_id=1, source_target_pairs={{0,1},{1,2},{2,3},{3,0},{4,5},{5,6},{6,7},{7,4},{8,9},{9,10},{10,1... | collective-permute-start | bytes 1572872 | tf_op jit(solution)/shard_map/ppermute | solution.py:235
  11.0 25.3 %collective-permute-start.5 = (f32[2,2,64,512]{3,2,1,0:T(8,128)S(1)}, f32[2,2,64,512]{3,2,1,0:T(8,128)}, u32[]{:S(2)}, u32[]{:S(2)}) collective-permute-start(f32[2,2,64,512]{3,2,1,0:T(8,128)S(1)} %copy-done.11), channel_id=1, source_target_pairs={{0,3},{1,0},{2,1},{3,2},{4,7},{5,4},{6,5},{7,6},{8,11},{9,8},{10,9... | collective-permute-start | bytes 1572872 | tf_op jit(solution)/shard_map/ppermute | solution.py:235
  22.6 5.5 %copy-start.1 = (f32[8,104,256]{2,1,0:T(8,128)}, f32[8,104,256]{2,1,0:T(8,128)S(1)}, u32[]{:S(2)}) copy-start(f32[8,104,256]{2,1,0:T(8,128)S(1)} %all-to-all-done.block_ref.own_ref) | copy-start | bytes 2555908
  28.1 9.5 %copy-start.7 = (f32[512,8,104]{0,2,1:T(8,128)S(1)}, f32[512,8,104]{0,2,1:T(8,128)}, u32[]{:S(2)}) copy-start(f32[512,8,104]{0,2,1:T(8,128)} %constant.82) | copy-start | bytes 5111812
  28.1 16.2 %all-to-all-start.1 = ((f32[8,96,256]{2,1,0:T(8,128)}), f32[8,96,256]{2,1,0:T(8,128)S(1)}, u32[]{:S(2)}, u32[]{:S(2)}) async-start(f32[8,96,256]{2,1,0:T(8,128)} %shard_map.86), calls=%async_computation.1 | async-start | bytes 1572864 | tf_op jit(solution)/shard_map/all_to_all | solution.py:259
  40.4 8.2 %copy-start = (f32[4,128,1024]{2,1,0:T(8,128)S(1)}, f32[4,128,1024]{2,1,0:T(8,128)}, u32[]{:S(2)}) copy-start(f32[4,128,1024]{2,1,0:T(8,128)} %own_ref.1) | copy-start | bytes 6291460
  44.3 4.4 %copy-start.8 = (f32[8,96,256]{2,1,0:T(8,128)}, f32[8,96,256]{2,1,0:T(8,128)S(1)}, u32[]{:S(2)}) copy-start(f32[8,96,256]{2,1,0:T(8,128)S(1)} %all-to-all-done.1) | copy-start | bytes 2359300
  44.3 38.8 %all-to-all-start.2 = ((f32[8,104,512]{2,1,0:T(8,128)}), f32[8,104,512]{2,1,0:T(8,128)}, u32[]{:S(2)}, u32[]{:S(2)}) async-start(f32[8,104,512]{2,1,0:T(8,128)} %fusion.40), calls=%async_computation.2 | async-start | bytes 3407872 | tf_op jit(solution)/shard_map/all_to_all | solution.py:248
  48.6 27.8 %copy-start.4 = (f32[512,768]{1,0:T(8,128)S(1)}, f32[512,768]{1,0:T(8,128)}, u32[]{:S(2)}) copy-start(f32[512,768]{1,0:T(8,128)} %constant.79.clone.table_ref) | copy-start | bytes 4718596
  48.7 22.4 %collective-permute-start = (f32[4,2,1024]{2,1,0:T(2,128)S(1)}, f32[4,2,1024]{2,1,0:T(2,128)S(1)}, u32[]{:S(2)}, u32[]{:S(2)}) collective-permute-start(f32[4,2,1024]{2,1,0:T(2,128)S(1)} %get-tuple-element.7), channel_id=1, source_target_pairs={{0,4},{4,8},{8,12},{12,16},{16,20},{20,24},{24,28},{28,0},{1,5},{5... | collective-permute-start | bytes 98312 | tf_op jit(solution)/shard_map/ppermute | solution.py:235
  49.1 22.0 %collective-permute-start.1 = (f32[4,2,1024]{2,1,0:T(2,128)S(1)}, f32[4,2,1024]{2,1,0:T(2,128)S(1)}, u32[]{:S(2)}, u32[]{:S(2)}) collective-permute-start(f32[4,2,1024]{2,1,0:T(2,128)S(1)} %get-tuple-element.6), channel_id=1, source_target_pairs={{0,28},{4,0},{8,4},{12,8},{16,12},{20,16},{24,20},{28,24},{1,29},{... | collective-permute-start | bytes 98312 | tf_op jit(solution)/shard_map/ppermute | solution.py:235
  72.6 28.8 %collective-permute-start.2 = (f32[264,1024]{1,0:T(8,128)}, f32[264,1024]{1,0:T(8,128)S(1)}, u32[]{:S(2)}, u32[]{:S(2)}) collective-permute-start(f32[264,1024]{1,0:T(8,128)} %get-tuple-element.4), channel_id=1, source_target_pairs={{0,1},{1,2},{2,3},{3,0},{4,5},{5,6},{6,7},{7,4},{8,9},{9,10},{10,1... | collective-permute-start | bytes 3244040 | tf_op jit(solution)/shard_map/ppermute | solution.py:235
  74.1 48.8 %collective-permute-start.3 = (f32[264,1024]{1,0:T(8,128)}, f32[264,1024]{1,0:T(8,128)}, u32[]{:S(2)}, u32[]{:S(2)}) collective-permute-start(f32[264,1024]{1,0:T(8,128)} %get-tuple-element.5), channel_id=1, source_target_pairs={{0,3},{1,0},{2,1},{3,2},{4,7},{5,4},{6,5},{7,6},{8,11},{9,8},{10,9... | collective-permute-start | bytes 3244040 | tf_op jit(solution)/shard_map/ppermute | solution.py:235
  76.4 5.1 %copy-start.9 = (f32[8,96,256]{2,1,0:T(8,128)S(1)}, f32[8,96,256]{2,1,0:T(8,128)}, u32[]{:S(2)}) copy-start(f32[8,96,256]{2,1,0:T(8,128)} %copy-done.8) | copy-start | bytes 2359300
  76.4 5.1 %copy-start.10 = (f32[512,8,96]{0,2,1:T(8,128)S(1)}, f32[512,8,96]{0,2,1:T(8,128)}, u32[]{:S(2)}) copy-start(f32[512,8,96]{0,2,1:T(8,128)} %constant.83) | copy-start | bytes 4718596
  81.5 1.6 %copy-start.5 = (f32[144,104]{1,0:T(8,128)S(1)}, f32[144,104]{1,0:T(8,128)}, u32[]{:S(2)}) copy-start(f32[144,104]{1,0:T(8,128)} %constant.80.clone.matrix_y_ref) | copy-start | bytes 179716
  83.1 1.2 copy-start.2
  84.3 1.6 %copy-start.6 = (f32[512,1024]{1,0:T(8,128)S(1)}, f32[512,1024]{1,0:T(8,128)}, u32[]{:S(2)}) copy-start(f32[512,1024]{1,0:T(8,128)} %fusion.synth_ref) | copy-start | bytes 6291460
